TPU v7x, 32 devices: a whole 2x2x4 slice. The times are simulated.
32 devices in a mesh: dp: 16 (over z, y, x), tensor: 2 (over core).
Axes of the slice: x: 2, y: 2, z: 4, core: 2. Of those that a mesh axis runs over, the one named last changes fastest.
Arguments:
- layer_in: bfloat16 [32768, 768], P(('dp', 'tensor')), may hold values from -6 to 6
- upstream: bfloat16 [32768, 768], P(('dp', 'tensor')), may hold values from -6 to 6
- lengths: int32 [32], P('dp'), may hold values from 256 to 1024, as said below
- rescale: float32 [768], replicated, may hold values from 0.5 to 1.5
- gating: bfloat16 [768, 1536], P('dp', 'tensor'), may hold values from -0.21875 to 0.21875
- content: bfloat16 [768, 1536], P('dp', 'tensor'), may hold values from -0.21875 to 0.21875
- selector: bfloat16 [768, 128], P('dp'), may hold values from -0.21875 to 0.21875
- timestep: bfloat16 [768, 24], P('dp', 'tensor'), may hold values from -0.21875 to 0.21875
- filters: float32 [4, 1536], P(None, 'tensor'), may hold values from -3 to 3
- kernels: float32 [4, 128], replicated, may hold values from -3 to 3
- biases: float32 [24], P('tensor'), may hold values from -6 to -2
- decays: float32 [24], P('tensor'), may hold values from -1 to 2
- shortcut: float32 [24], P('tensor'), may hold values from 0.5 to 1.5
- amplitude: float32 [1536], P('tensor'), may hold values from 0.5 to 1.5
- outgoing: bfloat16 [1536, 768], P('tensor', 'dp'), may hold values from -0.15625 to 0.15625
Outputs:
- layer_out: bfloat16 [32768, 768], P(('dp', 'tensor'))
- input_grad: bfloat16 [32768, 768], P(('dp', 'tensor'))
- rescale_grad: float32 [768], replicated
- gating_grad: float32 [768, 1536], P('dp', 'tensor')
- content_grad: float32 [768, 1536], P('dp', 'tensor')
- selector_grad: float32 [768, 128], P('dp')
- timestep_grad: float32 [768, 24], P('dp', 'tensor')
- filters_grad: float32 [4, 1536], P(None, 'tensor')
- kernels_grad: float32 [4, 128], replicated
- biases_grad: float32 [24], P('tensor')
- decays_grad: float32 [24], P('tensor')
- shortcut_grad: float32 [24], P('tensor')
- amplitude_grad: float32 [1536], P('tensor')
- outgoing_grad: float32 [1536, 768], P('tensor', 'dp')
Inputs may be any that keep to these rules, and one draw needn't show every extreme that they name: lengths[s] is the number of valid tokens of sequence s; in every draw some sequence fills all 1024 of its slots.
All inputs are finite; a program needn't handle non-finite values.
Results may differ from a plain program's by a relative error of at most 0.011.
Values may be sent and summed in bfloat16 or wider, within the bound.
No kernel may reach another device: no remote copies, remote signals or barrier semaphores. Data moves between devices by JAX's collectives and lax.ppermute only.
A program may use at most 256 MiB of HBM per device.

v0:
```python
import functools
import jax
import jax.numpy as jnp
from jax import lax
from jax.sharding import PartitionSpec as P

INNER_WIDTH = 1536
BLOCK_ROWS = 128
epsilon = 1e-05
precise = lax.Precision.HIGHEST


def causal_conv(values, kernel):
    taps = kernel.shape[0]
    length = values.shape[0]
    padded = jnp.pad(values, ((taps - 1, 0), (0, 0)))
    summed = jnp.zeros_like(values)
    for offset in range(taps):
        summed = summed + padded[offset : offset + length] * kernel[offset]
    return summed


def prepare(mask_full, values_in, select_in, step_in, filters, kernels, biases):
    values_act = jax.nn.silu(causal_conv(values_in, filters)) * mask_full[:, None]
    select_act = jax.nn.silu(causal_conv(select_in, kernels))
    step_sizes = jax.nn.softplus(step_in + biases)
    return (values_act, select_act, step_sizes)


def mix_heads(values_low, select_low, step_sizes, decays, shortcut, gate_in):
    length = values_low.shape[0]
    head_count = step_sizes.shape[1]
    head_width = values_low.shape[1] // head_count
    state_size = select_low.shape[1] // 2
    block_count = length // BLOCK_ROWS
    b_rows = select_low[:, :state_size].reshape(block_count, BLOCK_ROWS, state_size)
    c_rows = select_low[:, state_size:].reshape(block_count, BLOCK_ROWS, state_size)
    head_values = values_low.reshape(block_count, BLOCK_ROWS, head_count, head_width)
    log_decay = (-jnp.exp(decays) * step_sizes).reshape(block_count, BLOCK_ROWS, head_count)
    inclusive = jnp.cumsum(log_decay, axis=1)
    exclusive = inclusive - log_decay
    block_total = inclusive[:, -1]
    inclusive_heads = inclusive.transpose(0, 2, 1)
    exclusive_heads = exclusive.transpose(0, 2, 1)
    places = jnp.arange(BLOCK_ROWS)
    below_mask = (places[:, None] > places[None, :])[None, None, :, :]
    above_mask = (places[:, None] < places[None, :])[None, None, :, :]
    ahead_log = jnp.where(
        below_mask, inclusive_heads[:, :, :, None] - inclusive_heads[:, :, None, :], -1e30
    )
    behind_log = jnp.where(
        above_mask, exclusive_heads[:, :, None, :] - exclusive_heads[:, :, :, None], -1e30
    )
    gram_rows = jnp.einsum("cis,cjs->cij", c_rows, b_rows, precision=precise)
    scaled = head_values * step_sizes.reshape(block_count, BLOCK_ROWS, head_count)[..., None]
    scaled_heads = scaled.transpose(0, 2, 1, 3)
    coupling = gram_rows[:, None, :, :] * (jnp.exp(ahead_log) + jnp.exp(behind_log))
    inner_part = jnp.einsum("chij,chjp->cihp", coupling, scaled_heads, precision=precise)
    decay_out = jnp.exp(block_total[:, None, :] - inclusive)
    decay_in = jnp.exp(exclusive)
    gained_ahead = jnp.einsum("cjh,cjs,cjhp->chsp", decay_out, b_rows, scaled, precision=precise)
    gained_behind = jnp.einsum("cjh,cjs,cjhp->chsp", decay_in, b_rows, scaled, precision=precise)
    carry_decay = jnp.exp(block_total)

    def carry_step(state_now, pieces_in):
        block_decay, gained_state = pieces_in
        return (block_decay[:, None, None] * state_now + gained_state, state_now)

    empty_state = jnp.zeros((head_count, state_size, head_width), jnp.float32)
    _, earlier_state = lax.scan(carry_step, empty_state, (carry_decay, gained_ahead))
    _, later_state = lax.scan(carry_step, empty_state, (carry_decay, gained_behind), reverse=True)
    from_earlier = (
        jnp.einsum("cis,chsp->cihp", c_rows, earlier_state, precision=precise)
        * jnp.exp(inclusive)[..., None]
    )
    from_later = (
        jnp.einsum("cis,chsp->cihp", c_rows, later_state, precision=precise)
        * jnp.exp(block_total[:, None, :] - exclusive)[..., None]
    )
    mixed_out = inner_part + from_earlier + from_later + shortcut[:, None] * head_values
    return mixed_out.reshape(length, head_count * head_width) * jax.nn.silu(gate_in)


def arrange(gathered, tensor_rank, bc_share):
    full_gate, full_values, full_select, full_step, full_out = gathered
    forward_cat = jnp.concatenate((full_gate, full_values, full_select, full_step), axis=1)
    own_select = lax.dynamic_slice_in_dim(full_select, tensor_rank * bc_share, bc_share, 1)
    backward_cat = jnp.concatenate((full_gate, full_values, own_select, full_step), axis=1)
    return (forward_cat, backward_cat, full_out)


def place_slice(piece, tensor_rank, parts):
    last_axis = piece.ndim - 1
    full_shape = piece.shape[:-1] + (piece.shape[-1] * parts,)
    return lax.dynamic_update_slice_in_dim(
        jnp.zeros(full_shape, jnp.float32), piece, tensor_rank * piece.shape[-1], last_axis
    )


def own_slice(summed, tensor_rank, width_own):
    return lax.dynamic_slice_in_dim(summed, tensor_rank * width_own, width_own, summed.ndim - 1)


def on_device(
    layer_in,
    upstream,
    lengths,
    rescale,
    gating,
    content,
    selector,
    timestep,
    filters,
    kernels,
    biases,
    decays,
    shortcut,
    amplitude,
    outgoing,
):
    parts = lax.axis_size("tensor")
    tensor_rank = lax.axis_index("tensor")
    micro_count = lengths.shape[0]
    half_rows = layer_in.shape[0] // micro_count
    length = half_rows * parts
    inner_local = gating.shape[1]
    head_local = timestep.shape[1]
    state_cols = selector.shape[1]
    bc_share = state_cols // parts
    first_only = (tensor_rank == 0).astype(jnp.float32)
    positions = jnp.arange(length)
    own_positions = tensor_rank * half_rows + jnp.arange(half_rows)
    outputs_list = []
    grads_list = []
    total_in = None
    total_out = None
    rescale_acc = jnp.zeros(rescale.shape, jnp.float32)
    filters_acc = jnp.zeros(filters.shape, jnp.float32)
    kernels_acc = jnp.zeros(kernels.shape, jnp.float32)
    biases_acc = jnp.zeros(biases.shape, jnp.float32)
    decays_acc = jnp.zeros(decays.shape, jnp.float32)
    shortcut_acc = jnp.zeros(shortcut.shape, jnp.float32)
    amplitude_acc = jnp.zeros(amplitude.shape, jnp.float32)
    for micro_step in range(micro_count):
        forward_cat, backward_cat, full_out = arrange(
            (
                lax.all_gather(gating, "dp", axis=0, tiled=True),
                lax.all_gather(content, "dp", axis=0, tiled=True),
                lax.all_gather(selector, "dp", axis=0, tiled=True),
                lax.all_gather(timestep, "dp", axis=0, tiled=True),
                lax.all_gather(outgoing, "dp", axis=1, tiled=True),
            ),
            tensor_rank,
            bc_share,
        )
        low_end = micro_step * half_rows
        tok_rows = layer_in[low_end : low_end + half_rows].astype(jnp.float32)
        seq_length = lengths[micro_step]
        mask_own = (own_positions < seq_length).astype(jnp.float32)
        mask_full = (positions < seq_length).astype(jnp.float32)
        inverse = lax.rsqrt(jnp.mean(tok_rows * tok_rows, axis=-1, keepdims=True) + epsilon)
        unit_rows = tok_rows * inverse
        normed = (unit_rows * rescale).astype(jnp.bfloat16)
        sequence = lax.all_gather(normed, "tensor", axis=0, tiled=True)
        projected = jnp.dot(sequence, forward_cat, preferred_element_type=jnp.float32)
        gate_in = projected[:, :inner_local]
        values_in = projected[:, inner_local : 2 * inner_local]
        select_in = projected[:, 2 * inner_local : 2 * inner_local + state_cols]
        step_in = projected[:, 2 * inner_local + state_cols :]
        prepared, prepare_back = jax.vjp(
            functools.partial(prepare, mask_full),
            values_in,
            select_in,
            step_in,
            filters,
            kernels,
            biases,
        )
        values_act, select_act, step_sizes = prepared
        values_low = lax.optimization_barrier(values_act.astype(jnp.bfloat16)).astype(jnp.float32)
        select_low = lax.optimization_barrier(select_act.astype(jnp.bfloat16)).astype(jnp.float32)
        gated_pre, mix_back = jax.vjp(
            mix_heads, values_low, select_low, step_sizes, decays, shortcut, gate_in
        )
        squares = lax.psum(jnp.sum(gated_pre * gated_pre, axis=-1), "tensor")
        out_scale = lax.rsqrt(squares / INNER_WIDTH + epsilon)[:, None]
        gated = (gated_pre * out_scale * amplitude).astype(jnp.bfloat16)
        branch = lax.psum_scatter(
            jnp.dot(gated, full_out, preferred_element_type=jnp.float32).astype(jnp.bfloat16),
            "tensor",
            scatter_dimension=0,
            tiled=True,
        ).astype(jnp.float32)
        outputs_list.append((mask_own[:, None] * (tok_rows + branch)).astype(jnp.bfloat16))
        grad_rows_out = (
            upstream[low_end : low_end + half_rows].astype(jnp.float32) * mask_own[:, None]
        )
        grad_branch = lax.all_gather(
            grad_rows_out.astype(jnp.bfloat16), "tensor", axis=0, tiled=True
        )
        grad_out_mb = jnp.einsum(
            "ri,rd->id", gated, grad_branch, preferred_element_type=jnp.float32
        )
        grad_gated = jnp.einsum(
            "rd,id->ri", grad_branch, full_out, preferred_element_type=jnp.float32
        )
        weighted = grad_gated * amplitude
        cross = lax.psum(jnp.sum(weighted * gated_pre, axis=-1), "tensor")
        grad_pre = out_scale * weighted - gated_pre * out_scale**3 * (cross / INNER_WIDTH)[:, None]
        amplitude_acc = amplitude_acc + jnp.sum(grad_gated * gated_pre * out_scale, axis=0)
        grad_values_low, grad_select_part, grad_steps, grad_decays, grad_shortcut, grad_gate = (
            mix_back(grad_pre)
        )
        grad_select = lax.psum(grad_select_part.astype(jnp.bfloat16), "tensor").astype(jnp.float32)
        grad_values_in, grad_select_in, grad_step_in, grad_filters, grad_kernels, grad_biases = (
            prepare_back((grad_values_low, grad_select, grad_steps))
        )
        grad_proj = jnp.concatenate(
            (grad_gate, grad_values_in, grad_select_in, grad_step_in), axis=1
        ).astype(jnp.bfloat16)
        own_part = lax.dynamic_slice_in_dim(
            grad_proj, 2 * inner_local + tensor_rank * bc_share, bc_share, 1
        )
        grad_back = jnp.concatenate(
            (
                grad_proj[:, : 2 * inner_local],
                own_part,
                grad_proj[:, 2 * inner_local + state_cols :],
            ),
            axis=1,
        )
        grad_in_mb = jnp.einsum(
            "rd,rc->dc", sequence, grad_proj, preferred_element_type=jnp.float32
        )
        grad_normed = lax.psum_scatter(
            jnp.einsum(
                "rc,dc->rd", grad_back, backward_cat, preferred_element_type=jnp.float32
            ).astype(jnp.bfloat16),
            "tensor",
            scatter_dimension=0,
            tiled=True,
        ).astype(jnp.float32)
        weighted_in = grad_normed * rescale
        grad_input = (
            grad_rows_out
            + inverse * weighted_in
            - unit_rows * inverse * jnp.mean(weighted_in * unit_rows, axis=-1, keepdims=True)
        )
        grads_list.append(grad_input.astype(jnp.bfloat16))
        rescale_acc = rescale_acc + jnp.sum(grad_normed * unit_rows, axis=0)
        filters_acc = filters_acc + grad_filters
        kernels_acc = kernels_acc + grad_kernels
        biases_acc = biases_acc + grad_biases
        decays_acc = decays_acc + grad_decays
        shortcut_acc = shortcut_acc + grad_shortcut
        share_in, share_out = (grad_in_mb, grad_out_mb)
        total_in = share_in if total_in is None else total_in + share_in
        total_out = share_out if total_out is None else total_out + share_out
    total_in, total_out = (
        lax.psum_scatter(total_in, "dp", scatter_dimension=0, tiled=True),
        lax.psum_scatter(total_out, "dp", scatter_dimension=1, tiled=True),
    )
    small_sums = lax.psum(
        (
            rescale_acc,
            kernels_acc * first_only,
            place_slice(filters_acc, tensor_rank, parts),
            place_slice(biases_acc, tensor_rank, parts),
            place_slice(decays_acc, tensor_rank, parts),
            place_slice(shortcut_acc, tensor_rank, parts),
            place_slice(amplitude_acc, tensor_rank, parts),
        ),
        ("dp", "tensor"),
    )
    layer_out = jnp.concatenate(outputs_list, axis=0)
    input_grad = jnp.concatenate(grads_list, axis=0)
    gating_grad = total_in[:, :inner_local]
    content_grad = total_in[:, inner_local : 2 * inner_local]
    selector_grad = total_in[:, 2 * inner_local : 2 * inner_local + state_cols]
    timestep_grad = total_in[
        :, 2 * inner_local + state_cols : 2 * inner_local + state_cols + head_local
    ]
    filters_grad = own_slice(small_sums[2], tensor_rank, inner_local)
    biases_grad = own_slice(small_sums[3], tensor_rank, head_local)
    decays_grad = own_slice(small_sums[4], tensor_rank, head_local)
    shortcut_grad = own_slice(small_sums[5], tensor_rank, head_local)
    amplitude_grad = own_slice(small_sums[6], tensor_rank, inner_local)
    return (
        layer_out,
        input_grad,
        small_sums[0],
        gating_grad,
        content_grad,
        selector_grad,
        timestep_grad,
        filters_grad,
        small_sums[1],
        biases_grad,
        decays_grad,
        shortcut_grad,
        amplitude_grad,
        total_out,
    )


def solution(mesh):
    return jax.shard_map(
        on_device,
        mesh=mesh,
        in_specs=(
            P(("dp", "tensor"), None),
            P(("dp", "tensor"), None),
            P("dp"),
            P(),
            P("dp", "tensor"),
            P("dp", "tensor"),
            P("dp", None),
            P("dp", "tensor"),
            P(None, "tensor"),
            P(),
            P("tensor"),
            P("tensor"),
            P("tensor"),
            P("tensor"),
            P("tensor", "dp"),
        ),
        out_specs=(
            P(("dp", "tensor"), None),
            P(("dp", "tensor"), None),
            P(),
            P("dp", "tensor"),
            P("dp", "tensor"),
            P("dp", None),
            P("dp", "tensor"),
            P(None, "tensor"),
            P(),
            P("tensor"),
            P("tensor"),
            P("tensor"),
            P("tensor"),
            P("tensor", "dp"),
        ),
        check_vma=False,
    )
```

profile of v0, /device:TPU:0, one launch (start us, length us, event | category | flops | bytes accessed | tf_op | source)
XLA Modules:
  0.0 1310.7 jit_solution(3207367767485504378)
XLA Ops:
  22.2 42.8 %all-gather = bf16[16,48,12]{1,2,0:T(8,128)(2,1)S(1)} all-gather(bf16[1,48,12]{1,2,0:T(8,128)(2,1)S(1)} %bitcast.647), channel_id=1, replica_groups=mesh['dp'=16,'tensor'=2] {'dp'}, dimensions={0}, use_global_device_ids=true | all-gather | bytes 19584 | tf_op jit(solution)/shard_map/all_gather | solution.py:150
  65.2 36.8 %all_gather.35 = bf16[768,128]{1,0:T(8,128)(2,1)S(1)} all-gather(bf16[48,128]{1,0:T(8,128)(2,1)S(1)} %copy-done.187), channel_id=1, replica_groups=mesh['dp'=16,'tensor'=2] {'dp'}, dimensions={0}, use_global_device_ids=true | all-gather | bytes 208896 | tf_op jit(solution)/shard_map/all_gather | solution.py:149
  104.0 39.9 %all-gather.13.cloned.1.call-done = bf16[768,768]{1,0:T(8,128)(2,1)} async-done(((bf16[48,768]{1,0:T(8,128)(2,1)}), bf16[768,768]{1,0:T(8,128)(2,1)}) %all-gather.13.cloned.1.call-update) | async-done | bytes 1179664 | tf_op jit(solution)/shard_map/all_gather | solution.py:148
  164.4 23.8 %fusion.373 = f32[8,128,12]{2,0,1:T(8,128)S(1)} fusion(f32[8,128,12]{2,0,1:T(8,128)S(1)} %copy.531), kind=kOutput, calls=%fused_computation.612 | output fusion | flops 1560576 | bytes 98304 | tf_op jit(solution)/shard_map/jvp(jit(cumsum))/reduce_window_sum | solution.py:40
  211.0 13.0 multiply_convert_fusion.3
  240.2 29.2 %while.138 = (s32[]{:T(128)}, f32[12,64,64]{2,1,0:T(8,128)}, f32[8,12,64,64]{3,2,1,0:T(8,128)}, f32[8,12,1,1]{1,3,2,0:T(1,128)S(1)}, f32[8,12]{1,0:T(8,128)S(1)}...) while((s32[]{:T(128)}, f32[12,64,64]{2,1,0:T(8,128)}, f32[8,12,64,64]{3,2,1,0:T(8,128)}, ...), condition=%wide.region_12.14_spmd.clone, body=%wide.region_11.13_spmd.clone.sunk | while | flops 196611 | bytes 1378044 | solution.py:70
  283.9 29.1 %while.139 = (s32[]{:T(128)}, f32[12,64,64]{2,1,0:T(8,128)}, f32[8,12,64,64]{3,2,1,0:T(8,128)}, f32[8,12,1,1]{1,3,2,0:T(1,128)S(1)}, f32[8,12]{1,0:T(8,128)S(1)}...) while((s32[]{:T(128)}, f32[12,64,64]{2,1,0:T(8,128)}, ...), condition=%wide.region_14.16_spmd.clone, body=%wide.region_13.15_spmd.clone.sunk | while | flops 196612 | bytes 1377556 | solution.py:71
  330.1 16.8 %fusion.97 = f32[8,128,12,64]{1,3,2,0:T(8,128)S(1)} fusion(f32[8,128,12,64]{1,3,2,0:T(8,128)} %bitcast.600, f32[8,128,12,64]{1,3,2,0:T(8,128)} %bitcast.598, f32[8,128,12,64]{1,0,3,2:T(8,128)S(1)} %bitcast.567, f32[8,12,128]{2,1,0:T(8,128)} %copy.535, f32[8,12,128]{2,1,0:T(8,128)} %copy.532, f32[8,128,128]{2,1,0:T(8,128)} %fusion.289, ...), kind=kOutput, calls=%fused_computation.181 | convolution fusion | flops 1222901760 | bytes 13385776 | tf_op jit(solution)/shard_map/jvp(chij,chjp->cihp)/dot_general | solution.py:58
  366.2 28.9 %while.136 = (s32[]{:T(128)}, f32[12,64,64]{2,1,0:T(8,128)}, f32[8,12,64,64]{3,2,1,0:T(8,128)}, f32[8,12,1,1]{1,3,2,0:T(1,128)S(1)}, f32[8,12]{1,0:T(8,128)S(1)}...) while((s32[]{:T(128)}, f32[12,64,64]{2,1,0:T(8,128)}, f32[8,12,64,64]{3,2,1,0:T(8,128)}, ...), condition=%wide.region_3.5_spmd.clone, body=%wide.region_2.4_spmd.clone.sunk | while | flops 196611 | bytes 1378044 | solution.py:70
  399.9 8.0 fusion.34
  409.9 15.4 %while.137 = (s32[]{:T(128)}, f32[12,64,64]{2,1,0:T(8,128)S(1)}, f32[8,12,64,64]{3,2,1,0:T(8,128)}, f32[8,12,1,1]{1,3,2,0:T(1,128)S(1)}, f32[8,12]{1,0:T(8,128)S...) while((s32[]{:T(128)}, f32[12,64,64]{2,1,0:T(8,128)S(1)}, ...), condition=%wide.region_5.7_spmd.clone, body=%wide.region_4.6_spmd.clone.sunk | while | flops 196612 | bytes 1180948 | solution.py:71
  440.0 16.3 %fusion.101 = f32[8,128,12,64]{1,3,2,0:T(8,128)S(1)} fusion(f32[8,128,12,64]{1,3,2,0:T(8,128)} %bitcast.604, f32[8,128,12,64]{1,3,2,0:T(8,128)} %bitcast.602, f32[8,128,12,64]{1,0,3,2:T(8,128)S(1)} %bitcast.574, f32[8,12,128]{2,1,0:T(8,128)S(1)} %copy.508, f32[8,12,128]{2,1,0:T(8,128)S(1)} %copy.505, f32[8,128,128]{2,1,0:T(8,128)} %fusion.298, ...), kind=kOutput, calls=%fused_computation.186 | convolution fusion | flops 1222901760 | bytes 13385776 | tf_op jit(solution)/shard_map/jvp(chij,chjp->cihp)/dot_general | solution.py:58
  475.2 8.3 multiply_reduce_fusion.3
  486.0 13.8 %fusion.64 = (f32[768]{0:T(1024)}, f32[1024,768]{0,1:T(8,128)S(1)}, bf16[1024,768]{0,1:T(8,128)(2,1)}, bf16[1024,768]{0,1:T(8,128)(2,1)}, f32[768]{0:T(1024)}, /*index=5*/f32[1024,768]{0,1:T(8,128)S(1)}) fusion(bf16[1024,768]{0,1:T(8,128)(2,1)} %get-tuple-element.1362, f32[1024,1676]{0,1:T(8,128)} %copy-done.24, f32[1024]{0:T(1024)S(1)} %broadcast_multiply_fusion.19, ...), kind=kLoop, calls=%fused_computation.123 | loop fusion | flops 33028608 | bytes 37782528 | tf_op jit(solution)/shard_map/transpose(jvp())/reduce_sum | solution.py:80
  507.9 10.3 fusion.20
  526.2 10.1 fusion.14
  540.4 12.5 fusion.84
  555.0 51.9 %while.140 = (s32[]{:T(128)}, f32[12,64,64]{2,1,0:T(8,128)}, f32[8,12]{1,0:T(8,128)S(1)}, f32[8,12,64,64]{3,2,1,0:T(8,128)}, f32[8,12,64,64]{2,3,1,0:T(8,128)}, ...) while((s32[]{:T(128)}, f32[12,64,64]{2,1,0:T(8,128)}, ...), condition=%wide.region_22.24_spmd.clone, body=%wide.region_20.23_spmd.clone.sunk | while | flops 294903 | bytes 2556824 | solution.py:71
  606.9 8.2 fusion.32
  627.5 51.8 %while.142 = (s32[]{:T(128)}, f32[12,64,64]{2,1,0:T(8,128)}, f32[8,12]{1,0:T(8,128)S(1)}, f32[8,12,64,64]{3,2,1,0:T(8,128)}, f32[8,12,64,64]{2,3,1,0:T(8,128)}, ...) while((s32[]{:T(128)}, f32[12,64,64]{2,1,0:T(8,128)}, ...), condition=%wide.region_44.46_spmd.clone, body=%wide.region_42.45_spmd.clone.sunk | while | flops 294903 | bytes 2556824 | solution.py:71
  679.3 8.4 fusion.24
  696.0 51.5 %while.141 = (s32[]{:T(128)}, f32[12,64,64]{2,1,0:T(8,128)}, f32[8,12]{1,0:T(8,128)S(1)}, f32[8,12,64,64]{3,2,1,0:T(8,128)}, f32[8,12,64,64]{2,3,1,0:T(8,128)}, ...) while((s32[]{:T(128)}, f32[12,64,64]{2,1,0:T(8,128)}, ...), condition=%wide.region_25.27_spmd.clone, body=%wide.region_23.26_spmd.clone.sunk | while | flops 294904 | bytes 2556336 | solution.py:70
  747.5 12.4 multiply_reduce_fusion.15
  765.8 51.8 %while.143 = (s32[]{:T(128)}, f32[12,64,64]{2,1,0:T(8,128)}, f32[8,12]{1,0:T(8,128)S(1)}, f32[8,12,64,64]{3,2,1,0:T(8,128)}, f32[8,12,64,64]{2,3,1,0:T(8,128)}, ...) while((s32[]{:T(128)}, f32[12,64,64]{2,1,0:T(8,128)}, ...), condition=%wide.region_47.49_spmd.clone, body=%wide.region_45.48_spmd.clone.sunk | while | flops 294904 | bytes 2556336 | solution.py:70
  817.6 10.1 fusion.83
  838.3 27.9 %fusion.43 = (f32[8,12,128]{2,1,0:T(8,128)}, f32[8,12,128]{2,1,0:T(8,128)}, f32[8,12,128]{2,1,0:T(8,128)}, f32[8,12,128]{2,1,0:T(8,128)}, f32[8,128,128]{2,1,0:T...) fusion(f32[8,12,128]{2,1,0:T(8,128)S(1)} %copy-done.141, ...), kind=kOutput, calls=%fused_computation.89 | convolution fusion | flops 1258717184 | bytes 15351808 | tf_op jit(solution)/shard_map/transpose(jvp(chij,chjp->cihp))/dot_general | solution.py:58
  927.1 8.5 broadcast_multiply_fusion
  943.4 8.7 fusion.76
  1002.0 9.4 convolution_add_fusion
  1023.1 41.6 %all-reduce.42 = (f32[768]{0:T(1024)}, f32[4,1536]{1,0:T(4,128)S(1)}, f32[4,128]{1,0:T(4,128)}, f32[24]{0:T(128)S(1)}, f32[24]{0:T(128)S(1)}, /*index=5*/f32[24]{0:T(128)S(1)}, f32[1536]{0:T(1024)S(1)}) all-reduce(f32[768]{0:T(1024)S(1)} %add.463, ...), channel_id=1, replica_groups=mesh['dp'=16,'tensor'=2] {'dp','tensor'}, use_global_device_ids=true, to_apply=%region_64.66 | all-reduce | flops 9032 | bytes 72256 | tf_op jit(solution)/shard_map/psum | solution.py:263
  1073.4 97.9 %reduce-scatter.15.cloned.1.call-done = f32[48,1676]{1,0:T(8,128)} async-done(((f32[768,1676]{1,0:T(8,128)}), f32[48,1676]{1,0:T(8,128)}) %reduce-scatter.15.cloned.1.call-update) | async-done | bytes 321808 | tf_op jit(solution)/shard_map/reduce_scatter | solution.py:260
  1175.8 128.2 %reduce-scatter.17.cloned.1.call-done = f32[768,48]{0,1:T(8,128)} async-done(((f32[768,768]{0,1:T(8,128)}), f32[768,48]{0,1:T(8,128)}) %reduce-scatter.17.cloned.1.call-update) | async-done | bytes 147472 | tf_op jit(solution)/shard_map/reduce_scatter | solution.py:261
  (1074 shorter events, 679.9 us)
Async XLA Ops:
  7.2 96.8 %all-gather.17.cloned.1.call-start = ((), (), s32[]{:S(2)}) async-start(), calls=%async_computation.11 | async-start | bytes 2359296 | tf_op jit(solution)/shard_map/all_gather | solution.py:164
  12.7 52.5 %copy-start.187 = (bf16[48,128]{1,0:T(8,128)(2,1)S(1)}, bf16[48,128]{1,0:T(8,128)(2,1)}, u32[]{:S(2)}) copy-start(bf16[48,128]{1,0:T(8,128)(2,1)} %param.38) | copy-start | bytes 36868
  12.7 91.3 %all-gather.11.cloned.1.call-start = ((), (), s32[]{:S(2)}) async-start(), calls=%async_computation.7 | async-start | bytes 1253376 | tf_op jit(solution)/shard_map/all_gather | solution.py:147
  13.5 88.5 %copy-start.214 = (f32[12]{0:T(128)S(1)}, f32[12]{0:T(128)}, u32[]{:S(2)}) copy-start(f32[12]{0:T(128)} %param.43) | copy-start | bytes 148
  13.5 88.5 %copy-start.188 = (f32[4,768]{1,0:T(4,128)S(1)}, f32[4,768]{1,0:T(4,128)}, u32[]{:S(2)}) copy-start(f32[4,768]{1,0:T(4,128)} %param.40) | copy-start | bytes 36868
  13.5 130.4 %all-gather.13.cloned.1.call-start = ((), (), s32[]{:S(2)}) async-start(), calls=%async_computation.8 | async-start | bytes 1253376 | tf_op jit(solution)/shard_map/all_gather | solution.py:148
  14.2 88.4 %copy-start.207 = (f32[4,128]{1,0:T(4,128)S(1)}, f32[4,128]{1,0:T(4,128)}, u32[]{:S(2)}) copy-start(f32[4,128]{1,0:T(4,128)} %param.41) | copy-start | bytes 6148
  14.2 140.3 %all-gather.9.cloned.1.call-start = ((), (), s32[]{:S(2)}) async-start(), calls=%async_computation.6 | async-start | bytes 2359296 | tf_op jit(solution)/shard_map/all_gather | solution.py:164
  14.8 455.5 %all-gather.21.cloned.1.call-start = ((), (), s32[]{:S(2)}) async-start(), calls=%async_computation.15 | async-start | bytes 2359296 | tf_op jit(solution)/shard_map/all_gather | solution.py:198
  18.3 452.0 %all-gather.15.cloned.1.call-start = ((), (), s32[]{:S(2)}) async-start(), calls=%async_computation.9 | async-start | bytes 1253376 | tf_op jit(solution)/shard_map/all_gather | solution.py:151
  18.9 456.3 %all-gather.19.cloned.1.call-start = ((), (), s32[]{:S(2)}) async-start(), calls=%async_computation.13 | async-start | bytes 2359296 | tf_op jit(solution)/shard_map/all_gather | solution.py:198
  19.6 937.7 %all-reduce.48.cloned.1.call-start = ((), (), s32[]{:S(2)}) async-start(), calls=%async_computation.19 | async-start | bytes 1048576 | tf_op jit(solution)/shard_map/psum | solution.py:214
  65.2 89.4 %copy-start.107 = (bf16[16,48,12]{2,1,0:T(8,128)(2,1)}, bf16[16,48,12]{2,1,0:T(8,128)(2,1)S(1)}, u32[]{:S(2)}) copy-start(bf16[16,48,12]{2,1,0:T(8,128)(2,1)S(1)} %copy.690) | copy-start | bytes 55300
  102.0 56.9 %copy-start.205 = (f32[12]{0:T(128)}, f32[12]{0:T(128)S(1)}, u32[]{:S(2)}) copy-start(f32[12]{0:T(128)S(1)} %exponential_negate_fusion) | copy-start | bytes 148
  102.6 108.4 %copy-start.155 = (f32[768]{0:T(1024)}, f32[768]{0:T(1024)S(1)}, u32[]{:S(2)}) copy-start(f32[768]{0:T(1024)S(1)} %get-tuple-element.1221) | copy-start | bytes 9220
  102.6 108.4 %copy-start.157 = (f32[768]{0:T(1024)}, f32[768]{0:T(1024)S(1)}, u32[]{:S(2)}) copy-start(f32[768]{0:T(1024)S(1)} %get-tuple-element.1222) | copy-start | bytes 9220
  225.3 104.7 %copy-start = (f32[96,8,8,128]{3,2,1,0:T(8,128)}, f32[96,8,8,128]{3,2,1,0:T(8,128)S(1)}, u32[]{:S(2)}) copy-start(f32[96,8,8,128]{3,2,1,0:T(8,128)S(1)} %copy.724) | copy-start | bytes 9437188
  353.3 86.7 %copy-start.4 = (f32[96,8,8,128]{3,2,1,0:T(8,128)}, f32[96,8,8,128]{3,2,1,0:T(8,128)S(1)}, u32[]{:S(2)}) copy-start(f32[96,8,8,128]{3,2,1,0:T(8,128)S(1)} %copy.716) | copy-start | bytes 9437188
  437.6 70.3 %copy-start.144 = (f32[8,12,128]{2,1,0:T(8,128)}, f32[8,12,128]{2,1,0:T(8,128)S(1)}, u32[]{:S(2)}) copy-start(f32[8,12,128]{2,1,0:T(8,128)S(1)} %copy.508) | copy-start | bytes 147460
  437.7 63.1 %copy-start.91 = (f32[8,128,12]{1,2,0:T(8,128)}, f32[8,128,12]{1,2,0:T(8,128)S(1)}, u32[]{:S(2)}) copy-start(f32[8,128,12]{1,2,0:T(8,128)S(1)} %copy.519) | copy-start | bytes 147460
  440.0 67.9 %copy-start.140 = (f32[8,12,128]{2,1,0:T(8,128)}, f32[8,12,128]{2,1,0:T(8,128)S(1)}, u32[]{:S(2)}) copy-start(f32[8,12,128]{2,1,0:T(8,128)S(1)} %copy.505) | copy-start | bytes 147460
  500.5 35.8 %copy-start.7 = (f32[96,8,8,128]{3,2,1,0:T(8,128)}, f32[96,8,8,128]{3,2,1,0:T(8,128)S(1)}, u32[]{:S(2)}) copy-start(f32[96,8,8,128]{3,2,1,0:T(8,128)S(1)} %copy.721) | copy-start | bytes 9437188
  696.0 51.5 %copy-start.202 = (f32[12]{0:T(128)S(1)}, f32[12]{0:T(128)}, u32[]{:S(2)}) copy-start(f32[12]{0:T(128)} %param.44) | copy-start | bytes 148
  937.1 82.9 %reduce-scatter.13.cloned.1.call-start = ((), (), s32[]{:S(2)}) async-start(), calls=%async_computation.16 | async-start | bytes 2359296 | tf_op jit(solution)/shard_map/reduce_scatter | solution.py:235
  972.0 48.0 %reduce-scatter.11.cloned.1.call-start = ((), (), s32[]{:S(2)}) async-start(), calls=%async_computation.14 | async-start | bytes 2359296 | tf_op jit(solution)/shard_map/reduce_scatter | solution.py:235
  986.9 80.9 %reduce-scatter.9.cloned.1.call-start = ((), (), s32[]{:S(2)}) async-start(), calls=%async_computation.12 | async-start | bytes 2359296 | tf_op jit(solution)/shard_map/reduce_scatter | solution.py:188
  991.0 76.8 %reduce-scatter.7.cloned.1.call-start = ((), (), s32[]{:S(2)}) async-start(), calls=%async_computation.10 | async-start | bytes 2359296 | tf_op jit(solution)/shard_map/reduce_scatter | solution.py:188
  996.1 175.2 %reduce-scatter.15.cloned.1.call-start = ((), (), s32[]{:S(2)}) async-start(), calls=%async_computation.17 | async-start | bytes 5849088 | tf_op jit(solution)/shard_map/reduce_scatter | solution.py:260
  1011.4 292.6 %reduce-scatter.17.cloned.1.call-start = ((), (), s32[]{:S(2)}) async-start(), calls=%async_computation.18 | async-start | bytes 2506752 | tf_op jit(solution)/shard_map/reduce_scatter | solution.py:261
  1018.9 48.9 %copy-start.43 = (bf16[1024,768]{1,0:T(8,128)(2,1)S(1)}, bf16[1024,768]{1,0:T(8,128)(2,1)}, u32[]{:S(2)}) copy-start(bf16[1024,768]{1,0:T(8,128)(2,1)} %param.33) | copy-start | bytes 4718596
  1018.9 48.9 %copy-start.168 = (f32[512]{0:T(512)S(1)}, f32[512]{0:T(512)}, u32[]{:S(2)}) copy-start(f32[512]{0:T(512)} %copy-done.167) | copy-start | bytes 6148
  1019.0 48.9 %copy-start.170 = (f32[512]{0:T(512)S(1)}, f32[512]{0:T(512)}, u32[]{:S(2)}) copy-start(f32[512]{0:T(512)} %copy-done.169) | copy-start | bytes 6148
  (201 other events, 1218.7 us)
Sparse Core Ops, SparseCore 0:
  12.8 12.4 all-gather.16
  28.1 57.7 all-gather.10
  88.8 55.0 all-gather.12
  145.8 8.6 all-gather.8
  155.9 10.9 all-gather.20
  169.6 57.2 all-gather.14
  228.5 8.6 all-gather.18
  937.2 19.9 all-reduce.47
  972.2 10.2 reduce-scatter.12
  987.0 10.2 reduce-scatter.10
  999.6 10.2 reduce-scatter.8
  1012.0 10.3 reduce-scatter.6
  1028.5 142.8 reduce-scatter.14
  1177.4 126.5 reduce-scatter.16
where the time goes:
time: 1320 us; the launch traced here: 1310 us
  other arithmetic  348 us (26%)
  matrix products  304 us (23%)
  waiting for transfers between devices  276 us (21%)
  local copies, waits for them, and re-layouts  239 us (18%)
  blocking collectives  126 us (10%)
  between operations  16.9 us (1%)
    reduce_scatter x1, waiting for transfers between devices, on_device(): lax.psum_scatter(total_out, 'dp', scatter_dimension=1, tiled=True)  128 us
    reduce_scatter x1, waiting for transfers between devices, on_device(): lax.psum_scatter(total_in, 'dp', scatter_dimension=0, tiled=True)  97.9 us
    dot_general x6, matrix products, mix_heads(): jnp.einsum('chij,chjp->cihp', coupling, scaled_heads, precision=precise)  93.9 us
    dynamic_update_slice x64, other arithmetic, mix_heads(): lax.scan(carry_step, empty_state, (carry_decay, gained_ahead))  71 us
    reduce_sum x32, other arithmetic, carry_step(): return (block_decay[:, None, None] * state_now + gained_state, state_now)  66.1 us
    dynamic_slice x64, local copies, waits for them, and re-layouts, mix_heads(): lax.scan(carry_step, empty_state, (carry_decay, gained_ahead))  62.6 us
    add x32, other arithmetic, carry_step(): return (block_decay[:, None, None] * state_now + gained_state, state_now)  55.8 us
    dot_general x6, matrix products, mix_heads(): jnp.einsum('cjh,cjs,cjhp->chsp', decay_out, b_rows, scaled, precision=pre...  48.9 us
  transfers between devices with their start and end apart: 14, of which 5 were waited for; matrix products, arithmetic and copies ran while one was open for 31% of the time, Pallas kernels for 0%

commit v1 on v0

--- a/solution.py
+++ b/solution.py
@@ -261,16 +261,19 @@
         lax.psum_scatter(total_out, "dp", scatter_dimension=1, tiled=True),
     )
     small_sums = lax.psum(
-        (
-            rescale_acc,
-            kernels_acc * first_only,
-            place_slice(filters_acc, tensor_rank, parts),
-            place_slice(biases_acc, tensor_rank, parts),
-            place_slice(decays_acc, tensor_rank, parts),
-            place_slice(shortcut_acc, tensor_rank, parts),
-            place_slice(amplitude_acc, tensor_rank, parts),
+        lax.psum(
+            (
+                rescale_acc,
+                kernels_acc * first_only,
+                place_slice(filters_acc, tensor_rank, parts),
+                place_slice(biases_acc, tensor_rank, parts),
+                place_slice(decays_acc, tensor_rank, parts),
+                place_slice(shortcut_acc, tensor_rank, parts),
+                place_slice(amplitude_acc, tensor_rank, parts),
+            ),
+            "dp",
         ),
-        ("dp", "tensor"),
+        "tensor",
     )
     layer_out = jnp.concatenate(outputs_list, axis=0)
     input_grad = jnp.concatenate(grads_list, axis=0)

time: 1320 us -> 1320 us (level)
  blocking collectives: 126 us -> 166 us
  waiting for transfers between devices: 276 us -> 236 us
    reduce_scatter x1, waiting for transfers between devices: 97.9 us -> 57.4 us  [on_device(): lax.psum_scatter(total_in, 'dp', scatter_dimension=0, tiled=True)]
    psum x1, blocking collectives: 41.6 us -> 77.9 us  [on_device(): lax.psum((rescale_acc, kernels_acc * first_only, place_slice(filters_acc,...]
where the time goes in v1:
time: 1320 us; the launch traced here: 1310 us
  other arithmetic  348 us (26%)
  matrix products  304 us (23%)
  local copies, waits for them, and re-layouts  239 us (18%)
  waiting for transfers between devices  236 us (18%)
  blocking collectives  166 us (13%)
  between operations  16.9 us (1%)
    reduce_scatter x1, waiting for transfers between devices, on_device(): lax.psum_scatter(total_out, 'dp', scatter_dimension=1, tiled=True)  128 us
    dot_general x6, matrix products, mix_heads(): jnp.einsum('chij,chjp->cihp', coupling, scaled_heads, precision=precise)  93.9 us
    psum x1, blocking collectives, on_device(): lax.psum((rescale_acc, kernels_acc * first_only, place_slice(filters_acc,...  77.9 us
    dynamic_update_slice x64, other arithmetic, mix_heads(): lax.scan(carry_step, empty_state, (carry_decay, gained_ahead))  71.2 us
    reduce_sum x32, other arithmetic, carry_step(): return (block_decay[:, None, None] * state_now + gained_state, state_now)  66.2 us
    dynamic_slice x64, local copies, waits for them, and re-layouts, mix_heads(): lax.scan(carry_step, empty_state, (carry_decay, gained_ahead))  62.6 us
    reduce_scatter x1, waiting for transfers between devices, on_device(): lax.psum_scatter(total_in, 'dp', scatter_dimension=0, tiled=True)  57.4 us
    add x32, other arithmetic, carry_step(): return (block_decay[:, None, None] * state_now + gained_state, state_now)  55.9 us
  transfers between devices with their start and end apart: 14, of which 5 were waited for; matrix products, arithmetic and copies ran while one was open for 31% of the time, Pallas kernels for 0%

profile of v1, /device:TPU:0, one launch (start us, length us, event | category | flops | bytes accessed | tf_op | source)
XLA Modules:
  0.0 1310.7 jit_solution(6932351211631521330)
XLA Ops:
  22.2 42.8 %all-gather = bf16[16,48,12]{1,2,0:T(8,128)(2,1)S(1)} all-gather(bf16[1,48,12]{1,2,0:T(8,128)(2,1)S(1)} %bitcast.647), channel_id=1, replica_groups=mesh['dp'=16,'tensor'=2] {'dp'}, dimensions={0}, use_global_device_ids=true | all-gather | bytes 19584 | tf_op jit(solution)/shard_map/all_gather | solution.py:150
  65.2 36.8 %all_gather.35 = bf16[768,128]{1,0:T(8,128)(2,1)S(1)} all-gather(bf16[48,128]{1,0:T(8,128)(2,1)S(1)} %copy-done.187), channel_id=1, replica_groups=mesh['dp'=16,'tensor'=2] {'dp'}, dimensions={0}, use_global_device_ids=true | all-gather | bytes 208896 | tf_op jit(solution)/shard_map/all_gather | solution.py:149
  103.9 39.9 %all-gather.13.cloned.1.call-done = bf16[768,768]{1,0:T(8,128)(2,1)} async-done(((bf16[48,768]{1,0:T(8,128)(2,1)}), bf16[768,768]{1,0:T(8,128)(2,1)}) %all-gather.13.cloned.1.call-update) | async-done | bytes 1179664 | tf_op jit(solution)/shard_map/all_gather | solution.py:148
  164.4 23.8 %fusion.373 = f32[8,128,12]{2,0,1:T(8,128)S(1)} fusion(f32[8,128,12]{2,0,1:T(8,128)S(1)} %copy.531), kind=kOutput, calls=%fused_computation.612 | output fusion | flops 1560576 | bytes 98304 | tf_op jit(solution)/shard_map/jvp(jit(cumsum))/reduce_window_sum | solution.py:40
  211.1 13.0 multiply_convert_fusion.3
  240.3 29.2 %while.138 = (s32[]{:T(128)}, f32[12,64,64]{2,1,0:T(8,128)}, f32[8,12,64,64]{3,2,1,0:T(8,128)}, f32[8,12,1,1]{1,3,2,0:T(1,128)S(1)}, f32[8,12]{1,0:T(8,128)S(1)}...) while((s32[]{:T(128)}, f32[12,64,64]{2,1,0:T(8,128)}, f32[8,12,64,64]{3,2,1,0:T(8,128)}, ...), condition=%wide.region_12.14_spmd.clone, body=%wide.region_11.13_spmd.clone.sunk | while | flops 196611 | bytes 1378044 | solution.py:70
  274.0 8.0 fusion.26
  284.1 29.0 %while.139 = (s32[]{:T(128)}, f32[12,64,64]{2,1,0:T(8,128)}, f32[8,12,64,64]{3,2,1,0:T(8,128)}, f32[8,12,1,1]{1,3,2,0:T(1,128)S(1)}, f32[8,12]{1,0:T(8,128)S(1)}...) while((s32[]{:T(128)}, f32[12,64,64]{2,1,0:T(8,128)}, ...), condition=%wide.region_14.16_spmd.clone, body=%wide.region_13.15_spmd.clone.sunk | while | flops 196612 | bytes 1377556 | solution.py:71
  330.0 16.8 %fusion.97 = f32[8,128,12,64]{1,3,2,0:T(8,128)S(1)} fusion(f32[8,128,12,64]{1,3,2,0:T(8,128)} %bitcast.600, f32[8,128,12,64]{1,3,2,0:T(8,128)} %bitcast.598, f32[8,128,12,64]{1,0,3,2:T(8,128)S(1)} %bitcast.567, f32[8,12,128]{2,1,0:T(8,128)} %copy.535, f32[8,12,128]{2,1,0:T(8,128)} %copy.532, f32[8,128,128]{2,1,0:T(8,128)} %fusion.289, ...), kind=kOutput, calls=%fused_computation.181 | convolution fusion | flops 1222901760 | bytes 13385776 | tf_op jit(solution)/shard_map/jvp(chij,chjp->cihp)/dot_general | solution.py:58
  366.1 29.1 %while.136 = (s32[]{:T(128)}, f32[12,64,64]{2,1,0:T(8,128)}, f32[8,12,64,64]{3,2,1,0:T(8,128)}, f32[8,12,1,1]{1,3,2,0:T(1,128)S(1)}, f32[8,12]{1,0:T(8,128)S(1)}...) while((s32[]{:T(128)}, f32[12,64,64]{2,1,0:T(8,128)}, f32[8,12,64,64]{3,2,1,0:T(8,128)}, ...), condition=%wide.region_3.5_spmd.clone, body=%wide.region_2.4_spmd.clone.sunk | while | flops 196611 | bytes 1378044 | solution.py:70
  410.0 15.5 %while.137 = (s32[]{:T(128)}, f32[12,64,64]{2,1,0:T(8,128)S(1)}, f32[8,12,64,64]{3,2,1,0:T(8,128)}, f32[8,12,1,1]{1,3,2,0:T(1,128)S(1)}, f32[8,12]{1,0:T(8,128)S...) while((s32[]{:T(128)}, f32[12,64,64]{2,1,0:T(8,128)S(1)}, ...), condition=%wide.region_5.7_spmd.clone, body=%wide.region_4.6_spmd.clone.sunk | while | flops 196612 | bytes 1180948 | solution.py:71
  440.2 16.3 %fusion.101 = f32[8,128,12,64]{1,3,2,0:T(8,128)S(1)} fusion(f32[8,128,12,64]{1,3,2,0:T(8,128)} %bitcast.604, f32[8,128,12,64]{1,3,2,0:T(8,128)} %bitcast.602, f32[8,128,12,64]{1,0,3,2:T(8,128)S(1)} %bitcast.574, f32[8,12,128]{2,1,0:T(8,128)S(1)} %copy.508, f32[8,12,128]{2,1,0:T(8,128)S(1)} %copy.505, f32[8,128,128]{2,1,0:T(8,128)} %fusion.298, ...), kind=kOutput, calls=%fused_computation.186 | convolution fusion | flops 1222901760 | bytes 13385776 | tf_op jit(solution)/shard_map/jvp(chij,chjp->cihp)/dot_general | solution.py:58
  475.4 8.4 multiply_reduce_fusion.3
  486.2 13.8 %fusion.64 = (f32[768]{0:T(1024)}, f32[1024,768]{0,1:T(8,128)S(1)}, bf16[1024,768]{0,1:T(8,128)(2,1)}, bf16[1024,768]{0,1:T(8,128)(2,1)}, f32[768]{0:T(1024)}, /*index=5*/f32[1024,768]{0,1:T(8,128)S(1)}) fusion(bf16[1024,768]{0,1:T(8,128)(2,1)} %get-tuple-element.1369, f32[1024,1676]{0,1:T(8,128)} %copy-done.24, f32[1024]{0:T(1024)S(1)} %broadcast_multiply_fusion.19, ...), kind=kLoop, calls=%fused_computation.123 | loop fusion | flops 33028608 | bytes 37782528 | tf_op jit(solution)/shard_map/transpose(jvp())/reduce_sum | solution.py:80
  508.1 10.3 fusion.20
  526.4 10.1 fusion.14
  540.7 12.4 fusion.84
  555.2 51.9 %while.140 = (s32[]{:T(128)}, f32[12,64,64]{2,1,0:T(8,128)}, f32[8,12]{1,0:T(8,128)S(1)}, f32[8,12,64,64]{3,2,1,0:T(8,128)}, f32[8,12,64,64]{2,3,1,0:T(8,128)}, ...) while((s32[]{:T(128)}, f32[12,64,64]{2,1,0:T(8,128)}, ...), condition=%wide.region_22.24_spmd.clone, body=%wide.region_20.23_spmd.clone.sunk | while | flops 294903 | bytes 2556824 | solution.py:71
  607.2 8.2 fusion.32
  627.8 51.7 %while.142 = (s32[]{:T(128)}, f32[12,64,64]{2,1,0:T(8,128)}, f32[8,12]{1,0:T(8,128)S(1)}, f32[8,12,64,64]{3,2,1,0:T(8,128)}, f32[8,12,64,64]{2,3,1,0:T(8,128)}, ...) while((s32[]{:T(128)}, f32[12,64,64]{2,1,0:T(8,128)}, ...), condition=%wide.region_44.46_spmd.clone, body=%wide.region_42.45_spmd.clone.sunk | while | flops 294903 | bytes 2556824 | solution.py:71
  679.6 8.4 fusion.24
  696.3 51.7 %while.141 = (s32[]{:T(128)}, f32[12,64,64]{2,1,0:T(8,128)}, f32[8,12]{1,0:T(8,128)S(1)}, f32[8,12,64,64]{3,2,1,0:T(8,128)}, f32[8,12,64,64]{2,3,1,0:T(8,128)}, ...) while((s32[]{:T(128)}, f32[12,64,64]{2,1,0:T(8,128)}, ...), condition=%wide.region_25.27_spmd.clone, body=%wide.region_23.26_spmd.clone.sunk | while | flops 294904 | bytes 2556336 | solution.py:70
  748.0 12.4 multiply_reduce_fusion.15
  766.3 51.8 %while.143 = (s32[]{:T(128)}, f32[12,64,64]{2,1,0:T(8,128)}, f32[8,12]{1,0:T(8,128)S(1)}, f32[8,12,64,64]{3,2,1,0:T(8,128)}, f32[8,12,64,64]{2,3,1,0:T(8,128)}, ...) while((s32[]{:T(128)}, f32[12,64,64]{2,1,0:T(8,128)}, ...), condition=%wide.region_47.49_spmd.clone, body=%wide.region_45.48_spmd.clone.sunk | while | flops 294904 | bytes 2556336 | solution.py:70
  818.1 10.1 fusion.83
  838.8 27.9 %fusion.43 = (f32[8,12,128]{2,1,0:T(8,128)}, f32[8,12,128]{2,1,0:T(8,128)}, f32[8,12,128]{2,1,0:T(8,128)}, f32[8,12,128]{2,1,0:T(8,128)}, f32[8,128,128]{2,1,0:T...) fusion(f32[8,12,128]{2,1,0:T(8,128)S(1)} %copy-done.141, ...), kind=kOutput, calls=%fused_computation.89 | convolution fusion | flops 1258717184 | bytes 15351808 | tf_op jit(solution)/shard_map/transpose(jvp(chij,chjp->cihp))/dot_general | solution.py:58
  927.5 8.5 broadcast_multiply_fusion
  943.9 8.7 fusion.76
  1002.0 9.5 convolution_add_fusion
  1023.2 77.9 %all-reduce.42 = (f32[768]{0:T(1024)S(1)}, f32[4,1536]{1,0:T(4,128)S(1)}, f32[4,128]{1,0:T(4,128)S(1)}, f32[24]{0:T(128)S(1)}, f32[24]{0:T(128)S(1)}, /*index=5*/f32[24]{0:T(128)S(1)}, f32[1536]{0:T(1024)S(1)}) all-reduce(f32[768]{0:T(1024)S(1)} %add.477, ...), channel_id=1, replica_groups=mesh['dp'=16,'tensor'=2] {'dp'}, use_global_device_ids=true, to_apply=%region_64.66 | all-reduce | flops 9032 | bytes 72256 | tf_op jit(solution)/shard_map/psum | solution.py:264
  1113.8 57.4 %reduce-scatter.15.cloned.1.call-done = f32[48,1676]{1,0:T(8,128)} async-done(((f32[768,1676]{1,0:T(8,128)}), f32[48,1676]{1,0:T(8,128)}) %reduce-scatter.15.cloned.1.call-update) | async-done | bytes 321808 | tf_op jit(solution)/shard_map/reduce_scatter | solution.py:260
  1175.7 128.3 %reduce-scatter.17.cloned.1.call-done = f32[768,48]{0,1:T(8,128)} async-done(((f32[768,768]{0,1:T(8,128)}), f32[768,48]{0,1:T(8,128)}) %reduce-scatter.17.cloned.1.call-update) | async-done | bytes 147472 | tf_op jit(solution)/shard_map/reduce_scatter | solution.py:261
  (1073 shorter events, 683.8 us)
Async XLA Ops:
  7.2 96.7 %all-gather.17.cloned.1.call-start = ((), (), s32[]{:S(2)}) async-start(), calls=%async_computation.11 | async-start | bytes 2359296 | tf_op jit(solution)/shard_map/all_gather | solution.py:164
  12.7 52.5 %copy-start.187 = (bf16[48,128]{1,0:T(8,128)(2,1)S(1)}, bf16[48,128]{1,0:T(8,128)(2,1)}, u32[]{:S(2)}) copy-start(bf16[48,128]{1,0:T(8,128)(2,1)} %param.38) | copy-start | bytes 36868
  12.7 91.3 %all-gather.11.cloned.1.call-start = ((), (), s32[]{:S(2)}) async-start(), calls=%async_computation.7 | async-start | bytes 1253376 | tf_op jit(solution)/shard_map/all_gather | solution.py:147
  13.4 88.5 %copy-start.213 = (f32[12]{0:T(128)S(1)}, f32[12]{0:T(128)}, u32[]{:S(2)}) copy-start(f32[12]{0:T(128)} %param.43) | copy-start | bytes 148
  13.4 88.5 %copy-start.188 = (f32[4,768]{1,0:T(4,128)S(1)}, f32[4,768]{1,0:T(4,128)}, u32[]{:S(2)}) copy-start(f32[4,768]{1,0:T(4,128)} %param.40) | copy-start | bytes 36868
  13.5 130.4 %all-gather.13.cloned.1.call-start = ((), (), s32[]{:S(2)}) async-start(), calls=%async_computation.8 | async-start | bytes 1253376 | tf_op jit(solution)/shard_map/all_gather | solution.py:148
  14.2 88.4 %copy-start.207 = (f32[4,128]{1,0:T(4,128)S(1)}, f32[4,128]{1,0:T(4,128)}, u32[]{:S(2)}) copy-start(f32[4,128]{1,0:T(4,128)} %param.41) | copy-start | bytes 6148
  14.2 140.3 %all-gather.9.cloned.1.call-start = ((), (), s32[]{:S(2)}) async-start(), calls=%async_computation.6 | async-start | bytes 2359296 | tf_op jit(solution)/shard_map/all_gather | solution.py:164
  14.8 455.7 %all-gather.21.cloned.1.call-start = ((), (), s32[]{:S(2)}) async-start(), calls=%async_computation.15 | async-start | bytes 2359296 | tf_op jit(solution)/shard_map/all_gather | solution.py:198
  18.2 452.2 %all-gather.15.cloned.1.call-start = ((), (), s32[]{:S(2)}) async-start(), calls=%async_computation.9 | async-start | bytes 1253376 | tf_op jit(solution)/shard_map/all_gather | solution.py:151
  18.8 456.5 %all-gather.19.cloned.1.call-start = ((), (), s32[]{:S(2)}) async-start(), calls=%async_computation.13 | async-start | bytes 2359296 | tf_op jit(solution)/shard_map/all_gather | solution.py:198
  19.6 938.2 %all-reduce.49.cloned.1.call-start = ((), (), s32[]{:S(2)}) async-start(), calls=%async_computation.19 | async-start | bytes 1048576 | tf_op jit(solution)/shard_map/psum | solution.py:214
  65.2 89.4 %copy-start.107 = (bf16[16,48,12]{2,1,0:T(8,128)(2,1)}, bf16[16,48,12]{2,1,0:T(8,128)(2,1)S(1)}, u32[]{:S(2)}) copy-start(bf16[16,48,12]{2,1,0:T(8,128)(2,1)S(1)} %copy.690) | copy-start | bytes 55300
  101.9 56.9 %copy-start.205 = (f32[12]{0:T(128)}, f32[12]{0:T(128)S(1)}, u32[]{:S(2)}) copy-start(f32[12]{0:T(128)S(1)} %exponential_negate_fusion) | copy-start | bytes 148
  102.6 108.5 %copy-start.155 = (f32[768]{0:T(1024)}, f32[768]{0:T(1024)S(1)}, u32[]{:S(2)}) copy-start(f32[768]{0:T(1024)S(1)} %get-tuple-element.1221) | copy-start | bytes 9220
  102.6 108.5 %copy-start.157 = (f32[768]{0:T(1024)}, f32[768]{0:T(1024)S(1)}, u32[]{:S(2)}) copy-start(f32[768]{0:T(1024)S(1)} %get-tuple-element.1222) | copy-start | bytes 9220
  225.4 104.7 %copy-start = (f32[96,8,8,128]{3,2,1,0:T(8,128)}, f32[96,8,8,128]{3,2,1,0:T(8,128)S(1)}, u32[]{:S(2)}) copy-start(f32[96,8,8,128]{3,2,1,0:T(8,128)S(1)} %copy.724) | copy-start | bytes 9437188
  353.3 86.8 %copy-start.4 = (f32[96,8,8,128]{3,2,1,0:T(8,128)}, f32[96,8,8,128]{3,2,1,0:T(8,128)S(1)}, u32[]{:S(2)}) copy-start(f32[96,8,8,128]{3,2,1,0:T(8,128)S(1)} %copy.716) | copy-start | bytes 9437188
  437.8 70.3 %copy-start.144 = (f32[8,12,128]{2,1,0:T(8,128)}, f32[8,12,128]{2,1,0:T(8,128)S(1)}, u32[]{:S(2)}) copy-start(f32[8,12,128]{2,1,0:T(8,128)S(1)} %copy.508) | copy-start | bytes 147460
  437.8 63.1 %copy-start.91 = (f32[8,128,12]{1,2,0:T(8,128)}, f32[8,128,12]{1,2,0:T(8,128)S(1)}, u32[]{:S(2)}) copy-start(f32[8,128,12]{1,2,0:T(8,128)S(1)} %copy.519) | copy-start | bytes 147460
  440.2 67.9 %copy-start.140 = (f32[8,12,128]{2,1,0:T(8,128)}, f32[8,12,128]{2,1,0:T(8,128)S(1)}, u32[]{:S(2)}) copy-start(f32[8,12,128]{2,1,0:T(8,128)S(1)} %copy.505) | copy-start | bytes 147460
  500.7 35.8 %copy-start.7 = (f32[96,8,8,128]{3,2,1,0:T(8,128)}, f32[96,8,8,128]{3,2,1,0:T(8,128)S(1)}, u32[]{:S(2)}) copy-start(f32[96,8,8,128]{3,2,1,0:T(8,128)S(1)} %copy.721) | copy-start | bytes 9437188
  696.3 51.7 %copy-start.202 = (f32[12]{0:T(128)S(1)}, f32[12]{0:T(128)}, u32[]{:S(2)}) copy-start(f32[12]{0:T(128)} %param.44) | copy-start | bytes 148
  937.6 82.5 %reduce-scatter.13.cloned.1.call-start = ((), (), s32[]{:S(2)}) async-start(), calls=%async_computation.16 | async-start | bytes 2359296 | tf_op jit(solution)/shard_map/reduce_scatter | solution.py:235
  972.0 48.1 %reduce-scatter.11.cloned.1.call-start = ((), (), s32[]{:S(2)}) async-start(), calls=%async_computation.14 | async-start | bytes 2359296 | tf_op jit(solution)/shard_map/reduce_scatter | solution.py:235
  986.9 121.3 %reduce-scatter.9.cloned.1.call-start = ((), (), s32[]{:S(2)}) async-start(), calls=%async_computation.12 | async-start | bytes 2359296 | tf_op jit(solution)/shard_map/reduce_scatter | solution.py:188
  991.0 117.2 %reduce-scatter.7.cloned.1.call-start = ((), (), s32[]{:S(2)}) async-start(), calls=%async_computation.10 | async-start | bytes 2359296 | tf_op jit(solution)/shard_map/reduce_scatter | solution.py:188
  996.1 175.1 %reduce-scatter.15.cloned.1.call-start = ((), (), s32[]{:S(2)}) async-start(), calls=%async_computation.17 | async-start | bytes 5849088 | tf_op jit(solution)/shard_map/reduce_scatter | solution.py:260
  1011.5 292.5 %reduce-scatter.17.cloned.1.call-start = ((), (), s32[]{:S(2)}) async-start(), calls=%async_computation.18 | async-start | bytes 2506752 | tf_op jit(solution)/shard_map/reduce_scatter | solution.py:261
  1019.0 89.2 %copy-start.43 = (bf16[1024,768]{1,0:T(8,128)(2,1)S(1)}, bf16[1024,768]{1,0:T(8,128)(2,1)}, u32[]{:S(2)}) copy-start(bf16[1024,768]{1,0:T(8,128)(2,1)} %param.33) | copy-start | bytes 4718596
  1019.0 89.2 %copy-start.168 = (f32[512]{0:T(512)S(1)}, f32[512]{0:T(512)}, u32[]{:S(2)}) copy-start(f32[512]{0:T(512)} %copy-done.167) | copy-start | bytes 6148
  1019.0 89.2 %copy-start.170 = (f32[512]{0:T(512)S(1)}, f32[512]{0:T(512)}, u32[]{:S(2)}) copy-start(f32[512]{0:T(512)} %copy-done.169) | copy-start | bytes 6148
  (200 other events, 1212.7 us)
Sparse Core Ops, SparseCore 0:
  12.8 12.4 all-gather.16
  28.1 57.7 all-gather.10
  88.8 55.0 all-gather.12
  145.8 8.6 all-gather.8
  155.9 10.9 all-gather.20
  169.6 57.2 all-gather.14
  228.4 8.6 all-gather.18
  937.7 19.9 all-reduce.48
  972.1 10.2 reduce-scatter.12
  987.0 10.2 reduce-scatter.10
  999.6 10.2 reduce-scatter.8
  1012.0 10.2 reduce-scatter.6
  1028.4 142.7 reduce-scatter.14
  1177.3 126.5 reduce-scatter.16
